TPU v7x, 32 devices: a whole 2x2x4 slice. The times are simulated.
32 devices in a mesh: mem: 16 (over z, y, core), tile: 2 (over x).
Axes of the slice: x: 2, y: 2, z: 4, core: 2. Of those that a mesh axis runs over, the one named last changes fastest.
Arguments:
- member_perturbations: float32 [3, 32, 16, 256], P(None, 'mem', None, 'tile'), may hold values from -3 to 3
- obs_index: int32 [16, 2, 256], P('mem', 'tile'), may hold values from 0 to 383
- obs_value: float32 [16, 2, 256], P('mem', 'tile'), may hold values from -4 to 4
- obs_var: float32 [16, 2, 256], P('mem', 'tile'), may hold values from 0.05 to 0.5
- loc_weight: float32 [16, 2, 256], P('mem', 'tile'), may hold values from 0.2 to 1
Outputs:
- forecast: float32 [3, 32, 16, 256], P(None, 'mem', None, 'tile')
All inputs are finite; a program needn't handle non-finite values.
Results may differ from a plain program's by a relative error of at most 0.0003.
Values sent between devices are 32-bit elements; how exact they have to be, the bound alone decides.
A program may use at most 64 MiB of HBM per device.

v0:
```python
import jax
import jax.numpy as jnp
from jax import lax
from jax.sharding import PartitionSpec as P

PCELL = 128
NSIT = 6


mean_depth = 4.0
gravity = 0.25
coriolis = 0.1
time_step = 0.3
highest = lax.Precision.HIGHEST


def with_halo(cells, sides, width):
    for axis, dim in sides:
        count = lax.axis_size(axis)
        head = lax.slice_in_dim(cells, 0, width, axis=dim)
        tail = lax.slice_in_dim(cells, cells.shape[dim] - width, cells.shape[dim], axis=dim)
        cells = jnp.concatenate(
            [
                lax.ppermute(tail, axis, [(i, (i + 1) % count) for i in range(count)]),
                cells,
                lax.ppermute(head, axis, [((i + 1) % count, i) for i in range(count)]),
            ],
            axis=dim,
        )
    return cells


def middle(field):
    return field[..., 1:-1]


def across(field):
    return (field[..., 2:] - field[..., :-2]) * 0.5


def along(field):
    inner = middle(field)
    return (jnp.roll(inner, -1, -2) - jnp.roll(inner, 1, -2)) * 0.5


def tendency(extended):
    height = extended[0]
    east_wind = extended[1]
    north_wind = extended[2]
    depth_total = mean_depth + height
    east_mid = middle(east_wind)
    north_mid = middle(north_wind)
    d_height = -(across(depth_total * east_wind) + along(depth_total * north_wind))
    d_east = (
        -(east_mid * across(east_wind) + north_mid * along(east_wind))
        - gravity * across(height)
        + coriolis * north_mid
    )
    d_north = (
        -(east_mid * across(north_wind) + north_mid * along(north_wind))
        - gravity * along(height)
        - coriolis * east_mid
    )
    return jnp.stack([d_height, d_east, d_north])


def lead_interval_number(dynamics_variables):
    extended = with_halo(dynamics_variables, (("tile", 3),), 4)
    first_slope = tendency(extended)
    slope_two = tendency(extended[..., 1:-1] + 0.5 * time_step * first_slope)
    slope_three = tendency(extended[..., 2:-2] + 0.5 * time_step * slope_two)
    slope_four = tendency(extended[..., 3:-3] + time_step * slope_three)
    dynamics_variables = dynamics_variables + time_step / 6.0 * (
        first_slope[..., 3:-3]
        + 2.0 * slope_two[..., 2:-2]
        + 2.0 * slope_three[..., 1:-1]
        + slope_four
    )
    return dynamics_variables


def product(left, right):
    return jnp.einsum("rbij,rbjk->rbik", left, right, precision=highest)


def analyse(blocks, indices, values, variances, locality):
    members = blocks.shape[1]
    row_count = blocks.shape[2]
    block_count = blocks.shape[3]
    cells = blocks.shape[4]
    xbar = jnp.mean(blocks, axis=1, keepdims=True)
    pert = blocks - xbar
    flat = jnp.transpose(blocks, (2, 3, 0, 4, 1)).reshape(
        row_count, block_count, 3 * cells, members
    )
    observed = jnp.take_along_axis(flat, indices[..., None], axis=2)
    ybar = jnp.mean(observed, axis=3, keepdims=True)
    obs_pert = observed - ybar
    weighted = obs_pert * (locality / variances)[..., None]
    gram = jnp.einsum("rboi,rboj->rbij", weighted, obs_pert, precision=highest)
    identity = jnp.eye(members, dtype=jnp.float32)
    amat = gram + (members - 1.0) * identity
    frob = jnp.sqrt(jnp.sum(amat * amat, axis=(2, 3), keepdims=True))
    ymat = amat / frob
    zmat = jnp.broadcast_to(identity, amat.shape)
    for _ in range(NSIT):
        newton = 1.5 * identity - 0.5 * product(zmat, ymat)
        ymat = product(ymat, newton)
        zmat = product(newton, zmat)
    prec = product(zmat, zmat) / frob
    wmat = jnp.sqrt((members - 1.0) / frob) * zmat
    innov = values - ybar[..., 0]
    projected = jnp.einsum("rbok,rbo->rbk", weighted, innov, precision=highest)
    wbar = jnp.einsum("rbij,rbj->rbi", prec, projected, precision=highest)
    wtot = wmat + wbar[..., None]
    return xbar + jnp.einsum("virbc,rbij->vjrbc", pert, wtot, precision=highest)


def local(member_perturbations, obs_index, obs_value, obs_var, loc_weight):
    background_member_set = lead_interval_number(member_perturbations)
    patches = lax.all_to_all(background_member_set, "mem", split_axis=2, concat_axis=1, tiled=True)
    members = patches.shape[1]
    row_count = patches.shape[2]
    columns = patches.shape[3]
    blocks = patches.reshape(3, members, row_count, columns // PCELL, PCELL)
    updated_member_set = analyse(blocks, obs_index, obs_value, obs_var, loc_weight)
    closing_solution = lax.all_to_all(
        updated_member_set.reshape(3, members, row_count, columns),
        "mem",
        split_axis=1,
        concat_axis=2,
        tiled=True,
    )
    return lead_interval_number(closing_solution)


def solution(mesh):
    in_specs = (
        P(None, "mem", None, "tile"),
        P("mem", "tile", None),
        P("mem", "tile", None),
        P("mem", "tile", None),
        P("mem", "tile", None),
    )
    out_specs = P(None, "mem", None, "tile")
    return jax.shard_map(local, mesh=mesh, in_specs=in_specs, out_specs=out_specs, check_vma=False)
```

profile of v0, /device:TPU:0, one launch (start us, length us, event | category | flops | bytes accessed | tf_op | source)
XLA Modules:
  0.0 52.3 jit_solution(7982997128042682452)
XLA Ops:
  0.0 1.0 %fusion.239 = (f32[3,2,16,4]{3,2,1,0:T(8,128)S(1)}, f32[3,2,16,4]{3,2,1,0:T(8,128)S(1)}) fusion(f32[3,2,16,128]{3,2,1,0:T(8,128)} %param.5), kind=kLoop, calls=%fused_computation.385 | loop fusion | bytes 6144 | tf_op jit(solution)/shard_map/slice | solution.py:21
  1.0 3.0 %collective-permute-start = (f32[3,2,16,4]{3,2,1,0:T(8,128)S(1)}, f32[3,2,16,4]{3,2,1,0:T(8,128)S(1)}, u32[]{:S(2)}, u32[]{:S(2)}) collective-permute-start(f32[3,2,16,4]{3,2,1,0:T(8,128)S(1)} %get-tuple-element.59), channel_id=1, source_target_pairs={{0,1},{1,0},{2,3},{3,2},{4,5},{5,4},{6,7},{7,6},{8,9},{9,8},{10,11... | collective-permute-start | bytes 4616 | tf_op jit(solution)/shard_map/ppermute | solution.py:24
  4.1 0.7 %copy-done.2 = f32[1,1,256]{2,1,0:T(1,128)S(1)} copy-done((f32[1,1,256]{2,1,0:T(1,128)S(1)}, f32[1,1,256]{2,1,0:T(1,128)}, u32[]{:S(2)}) %copy-start.2) | copy-done | bytes 1048
  4.8 1.3 %collective-permute-done = f32[3,2,16,4]{3,2,1,0:T(8,128)S(1)} collective-permute-done((f32[3,2,16,4]{3,2,1,0:T(8,128)S(1)}, f32[3,2,16,4]{3,2,1,0:T(8,128)S(1)}, u32[]{:S(2)}, u32[]{:S(2)}) %collective-permute-start) | collective-permute-done | bytes 1568 | tf_op jit(solution)/shard_map/ppermute | solution.py:24
  6.1 2.0 %collective-permute-done.1 = f32[3,2,16,4]{3,2,1,0:T(8,128)S(1)} collective-permute-done((f32[3,2,16,4]{3,2,1,0:T(8,128)S(1)}, f32[3,2,16,4]{3,2,1,0:T(8,128)S(1)}, u32[]{:S(2)}, u32[]{:S(2)}) %collective-permute-start.1) | collective-permute-done | bytes 1568 | tf_op jit(solution)/shard_map/ppermute | solution.py:26
  12.4 0.7 %copy.57 = f32[3,2,16,128]{3,0,1,2:T(4,128)} copy(f32[3,2,16,128]{3,2,1,0:T(8,128)S(1)} %fusion.33) | data formatting | bytes 98304 | tf_op jit(solution)/shard_map/add | solution.py:73
  13.0 5.9 %all-to-all-start = ((f32[3,2,16,128]{3,0,1,2:T(4,128)}), f32[3,2,16,128]{3,0,1,2:T(4,128)S(1)}, u32[]{:S(2)}, u32[]{:S(2)}) async-start(f32[3,2,16,128]{3,0,1,2:T(4,128)} %copy.57), calls=%async_computation | async-start | bytes 131072 | tf_op jit(solution)/shard_map/all_to_all | solution.py:121
  19.0 6.9 %all-to-all-done = f32[3,2,16,128]{3,0,1,2:T(4,128)S(1)} async-done(((f32[3,2,16,128]{3,0,1,2:T(4,128)}), f32[3,2,16,128]{3,0,1,2:T(4,128)S(1)}, u32[]{:S(2)}, u32[]{:S(2)}) %all-to-all-start) | async-done | bytes 49184 | tf_op jit(solution)/shard_map/all_to_all | solution.py:121
  26.0 0.7 %gather_fusion = f32[256,32]{1,0:T(8,128)S(1)} fusion(f32[384,32]{1,0:T(8,128)S(1)} %bitcast.274, s32[1024]{0:T(1024)S(1)} %pad_clamp_fusion), kind=kCustom, calls=%fused_computation | custom fusion | bytes 66560 | tf_op jit(solution)/shard_map/jit(take_along_axis)/gather | solution.py:96
  26.8 0.2 fusion.13
  26.9 1.2 %multiply_reduce_fusion = (f32[]{:T(128)}, f32[32,32]{1,0:T(8,128)S(1)}) fusion(f32[256,32]{1,0:T(8,128)S(1)} %gather_fusion, f32[256]{0:T(256)S(1)} %broadcast_multiply_fusion.1, pred[256]{0:T(512)(128)(4,1)S(1)} %compare_and_fusion, f32[256]{0:T(256)S(1)} %bitcast.283), kind=kOutput, calls=%fused_computation.366 | convolution fusion | flops 3191807 | bytes 39172 | tf_op jit(solution)/shard_map/rboi,rboj->rbij/dot_general | solution.py:100
  29.7 0.2 fusion.5
  30.1 0.2 fusion.4
  30.6 0.2 fusion.3
  31.1 0.2 fusion.2
  31.7 0.7 %copy-done.4 = f32[1,1,256]{2,1,0:T(1,128)S(1)} copy-done((f32[1,1,256]{2,1,0:T(1,128)S(1)}, f32[1,1,256]{2,1,0:T(1,128)}, u32[]{:S(2)}) %copy-start.4) | copy-done | bytes 1048
  32.4 0.3 convolution_bitcast_fusion.2
  32.9 0.3 fusion.1
  33.3 9.3 %all_to_all.33 = f32[3,32,1,128]{3,2,0,1:T(1,128)S(1)} all-to-all(f32[3,32,1,128]{3,2,0,1:T(1,128)S(1)} %copy.62), channel_id=1, replica_groups=mesh['mem'=16,'tile'=2] {'mem'}, dimensions={1} | all-to-all | bytes 98304 | tf_op jit(solution)/shard_map/all_to_all | solution.py:127
  42.7 0.5 %collective-permute-start.2 = (f32[3,2,16,4]{3,2,1,0:T(8,128)S(1)}, f32[3,2,16,4]{3,2,1,0:T(8,128)S(1)}, u32[]{:S(2)}, u32[]{:S(2)}) collective-permute-start(f32[3,2,16,4]{3,2,1,0:T(8,128)S(1)} %get-tuple-element.57), channel_id=1, source_target_pairs={{0,1},{1,0},{2,3},{3,2},{4,5},{5,4},{6,7},{7,6},{8,9},{9,8},{10,11... | collective-permute-start | bytes 4616 | tf_op jit(solution)/shard_map/ppermute | solution.py:24
  43.3 1.5 %collective-permute-start.3 = (f32[3,2,16,4]{3,2,1,0:T(8,128)S(1)}, f32[3,2,16,4]{3,2,1,0:T(8,128)S(1)}, u32[]{:S(2)}, u32[]{:S(2)}) collective-permute-start(f32[3,2,16,4]{3,2,1,0:T(8,128)S(1)} %get-tuple-element.58), channel_id=1, source_target_pairs={{1,0},{0,1},{3,2},{2,3},{5,4},{4,5},{7,6},{6,7},{9,8},{8,9},{11,10... | collective-permute-start | bytes 4616 | tf_op jit(solution)/shard_map/ppermute | solution.py:26
  44.7 2.1 %collective-permute-done.2 = f32[3,2,16,4]{3,2,1,0:T(8,128)S(1)} collective-permute-done((f32[3,2,16,4]{3,2,1,0:T(8,128)S(1)}, f32[3,2,16,4]{3,2,1,0:T(8,128)S(1)}, u32[]{:S(2)}, u32[]{:S(2)}) %collective-permute-start.2) | collective-permute-done | bytes 1568 | tf_op jit(solution)/shard_map/ppermute | solution.py:24
  46.8 0.5 %collective-permute-done.3 = f32[3,2,16,4]{3,2,1,0:T(8,128)S(1)} collective-permute-done((f32[3,2,16,4]{3,2,1,0:T(8,128)S(1)}, f32[3,2,16,4]{3,2,1,0:T(8,128)S(1)}, u32[]{:S(2)}, u32[]{:S(2)}) %collective-permute-start.3) | collective-permute-done | bytes 1568 | tf_op jit(solution)/shard_map/ppermute | solution.py:26
  51.6 0.7 %fusion.28 = f32[3,2,16,128]{3,2,1,0:T(8,128)} fusion(f32[3,2,16,130]{3,2,1,0:T(8,128)S(1)} %get-tuple-element.11, f32[3,2,16,132]{3,2,1,0:T(8,128)S(1)} %get-tuple-element.14, f32[3,2,16,134]{3,2,1,0:T(8,128)S(1)} %get-tuple-element.12, f32[1,2,16,128]{3,2,1,0:T(8,128)S(1)} %fusion.185, f32[1,2,16,128]{3,2,1,0:T(8,128)S(1)} %fusion.189, ...), kind=kLoop, calls=%fused_computation.55 | loop fusion | flops 110592 | bytes 294912 | tf_op jit(solution)/shard_map/add | solution.py:73
  (150 shorter events, 10.9 us)
Async XLA Ops:
  0.0 8.1 %copy-start = (f32[3,2,16,128]{3,2,1,0:T(8,128)S(1)}, f32[3,2,16,128]{3,2,1,0:T(8,128)}, u32[]{:S(2)}) copy-start(f32[3,2,16,128]{3,2,1,0:T(8,128)} %param.5) | copy-start | bytes 147460
  1.0 3.1 %copy-start.3 = (s32[1,1,256]{2,1,0:T(1,128)S(1)}, s32[1,1,256]{2,1,0:T(1,128)}, u32[]{:S(2)}) copy-start(s32[1,1,256]{2,1,0:T(1,128)} %param.6) | copy-start | bytes 3076
  1.0 5.1 %collective-permute-start = (f32[3,2,16,4]{3,2,1,0:T(8,128)S(1)}, f32[3,2,16,4]{3,2,1,0:T(8,128)S(1)}, u32[]{:S(2)}, u32[]{:S(2)}) collective-permute-start(f32[3,2,16,4]{3,2,1,0:T(8,128)S(1)} %get-tuple-element.59), channel_id=1, source_target_pairs={{0,1},{1,0},{2,3},{3,2},{4,5},{5,4},{6,7},{7,6},{8,9},{9,8},{10,11... | collective-permute-start | bytes 4616 | tf_op jit(solution)/shard_map/ppermute | solution.py:24
  4.0 4.1 %collective-permute-start.1 = (f32[3,2,16,4]{3,2,1,0:T(8,128)S(1)}, f32[3,2,16,4]{3,2,1,0:T(8,128)S(1)}, u32[]{:S(2)}, u32[]{:S(2)}) collective-permute-start(f32[3,2,16,4]{3,2,1,0:T(8,128)S(1)} %get-tuple-element.60), channel_id=1, source_target_pairs={{1,0},{0,1},{3,2},{2,3},{5,4},{4,5},{7,6},{6,7},{9,8},{8,9},{11,10... | collective-permute-start | bytes 4616 | tf_op jit(solution)/shard_map/ppermute | solution.py:26
  4.1 0.7 %copy-start.2 = (f32[1,1,256]{2,1,0:T(1,128)S(1)}, f32[1,1,256]{2,1,0:T(1,128)}, u32[]{:S(2)}) copy-start(f32[1,1,256]{2,1,0:T(1,128)} %param.8) | copy-start | bytes 3076
  4.1 0.7 %copy-start.1 = (f32[1,1,256]{2,1,0:T(1,128)S(1)}, f32[1,1,256]{2,1,0:T(1,128)}, u32[]{:S(2)}) copy-start(f32[1,1,256]{2,1,0:T(1,128)} %param.9) | copy-start | bytes 3076
  13.0 12.8 %all-to-all-start = ((f32[3,2,16,128]{3,0,1,2:T(4,128)}), f32[3,2,16,128]{3,0,1,2:T(4,128)S(1)}, u32[]{:S(2)}, u32[]{:S(2)}) async-start(f32[3,2,16,128]{3,0,1,2:T(4,128)} %copy.57), calls=%async_computation | async-start | bytes 131072 | tf_op jit(solution)/shard_map/all_to_all | solution.py:121
  31.7 0.7 %copy-start.4 = (f32[1,1,256]{2,1,0:T(1,128)S(1)}, f32[1,1,256]{2,1,0:T(1,128)}, u32[]{:S(2)}) copy-start(f32[1,1,256]{2,1,0:T(1,128)} %param.7) | copy-start | bytes 3076
  42.7 4.1 %collective-permute-start.2 = (f32[3,2,16,4]{3,2,1,0:T(8,128)S(1)}, f32[3,2,16,4]{3,2,1,0:T(8,128)S(1)}, u32[]{:S(2)}, u32[]{:S(2)}) collective-permute-start(f32[3,2,16,4]{3,2,1,0:T(8,128)S(1)} %get-tuple-element.57), channel_id=1, source_target_pairs={{0,1},{1,0},{2,3},{3,2},{4,5},{5,4},{6,7},{7,6},{8,9},{9,8},{10,11... | collective-permute-start | bytes 4616 | tf_op jit(solution)/shard_map/ppermute | solution.py:24
  43.3 4.1 %collective-permute-start.3 = (f32[3,2,16,4]{3,2,1,0:T(8,128)S(1)}, f32[3,2,16,4]{3,2,1,0:T(8,128)S(1)}, u32[]{:S(2)}, u32[]{:S(2)}) collective-permute-start(f32[3,2,16,4]{3,2,1,0:T(8,128)S(1)} %get-tuple-element.58), channel_id=1, source_target_pairs={{1,0},{0,1},{3,2},{2,3},{5,4},{4,5},{7,6},{6,7},{9,8},{8,9},{11,10... | collective-permute-start | bytes 4616 | tf_op jit(solution)/shard_map/ppermute | solution.py:26
where the time goes:
time: 52.7 us; the launch traced here: 52.3 us
  waiting for transfers between devices  12.8 us (24%)
  starting transfers between devices  11.1 us (21%)
  blocking collectives  9.34 us (18%)
  local copies, waits for them, and re-layouts  9.04 us (17%)
  matrix products  4.63 us (9%)
  other arithmetic  4.22 us (8%)
  between operations  1.26 us (2%)
    all_to_all x1, blocking collectives, local(): lax.all_to_all(updated_member_set.reshape(3, members, row_count, columns)...  9.34 us
    all_to_all x1, waiting for transfers between devices, local(): lax.all_to_all(background_member_set, 'mem', split_axis=2, concat_axis=1,...  6.88 us
    all_to_all x1, starting transfers between devices, local(): lax.all_to_all(background_member_set, 'mem', split_axis=2, concat_axis=1,...  5.94 us
    slice x62, local copies, waits for them, and re-layouts, along(): return (jnp.roll(inner, -1, -2) - jnp.roll(inner, 1, -2)) * 0.5  4.91 us
    ppermute x2, starting transfers between devices, with_halo(): lax.ppermute(tail, axis, [(i, (i + 1) % count) for i in range(count)])  3.57 us
    ppermute x2, waiting for transfers between devices, with_halo(): lax.ppermute(tail, axis, [(i, (i + 1) % count) for i in range(count)])  3.35 us
    dot_general x18, matrix products, product(): return jnp.einsum('rbij,rbjk->rbik', left, right, precision=highest)  2.66 us
    another operation x28, other arithmetic, tendency(): return jnp.stack([d_height, d_east, d_north])  2.64 us
  transfers between devices with their start and end apart: 5, of which 5 were waited for; matrix products, arithmetic and copies ran while one was open for 0% of the time, Pallas kernels for 0%

commit v1 on v0

v1 whole, which is shorter than its diff:
```python
import functools

import jax
import jax.numpy as jnp
from jax import lax
from jax.experimental import pallas as pl
from jax.experimental.pallas import tpu as pltpu
from jax.sharding import PartitionSpec as P

PCELL = 128
NSIT = 6
HALO = 4

mean_depth = 4.0
gravity = 0.25
coriolis = 0.1
time_step = 0.3

MESH = pl.DeviceIdType.MESH
PAIRS = ((0, 0), (0, 1), (0, 2), (1, 0), (1, 1), (1, 2), (2, 0), (2, 1))


def across(field):
    width = field.shape[1]
    return (pltpu.roll(field, width - 1, 1) - pltpu.roll(field, 1, 1)) * 0.5


def along(field):
    rows = field.shape[0]
    return (pltpu.roll(field, rows - 1, 0) - pltpu.roll(field, 1, 0)) * 0.5


def tendency(fields):
    height, east, north = fields
    depth_total = mean_depth + height
    d_height = -(across(depth_total * east) + along(depth_total * north))
    d_east = -(east * across(east) + north * along(east)) - gravity * across(height) + coriolis * north
    d_north = -(east * across(north) + north * along(north)) - gravity * along(height) - coriolis * east
    return d_height, d_east, d_north


def advance(fields):
    def moved(scale, slopes):
        return [f + scale * s for f, s in zip(fields, slopes)]

    one = tendency(fields)
    two = tendency(moved(0.5 * time_step, one))
    total = [a + 2.0 * b for a, b in zip(one, two)]
    three = tendency(moved(0.5 * time_step, two))
    total = [a + 2.0 * b for a, b in zip(total, three)]
    four = tendency(moved(time_step, three))
    return [f + (time_step / 6.0) * (a + b) for f, a, b in zip(fields, total, four)]


def pieces(value):
    parts = []
    for _ in range(3):
        part = value.astype(jnp.bfloat16)
        parts.append(part)
        value = value - part.astype(jnp.float32)
    return parts


def left_factor(value, size):
    rep = 128 // size
    parts = [p.astype(jnp.float32) for p in pieces(value)]
    group = lax.broadcasted_iota(jnp.int32, value.shape, 1) // size
    tiles = []
    for first in range(0, len(PAIRS), rep):
        chosen = [parts[a] for a, _ in PAIRS[first : first + rep]]
        chosen += [jnp.zeros_like(value)] * (rep - len(chosen))
        tile = chosen[-1]
        for g in range(rep - 2, -1, -1):
            if chosen[g] is not chosen[g + 1]:
                tile = jnp.where(group <= g, chosen[g], tile)
        tiles.append(tile.astype(jnp.bfloat16))
    return jnp.concatenate(tiles, axis=1)


def right_factor(value, size):
    rep = 128 // size
    parts = pieces(value)
    stack = [parts[b] for _, b in PAIRS]
    stack += [parts[0]] * (-len(PAIRS) % rep)
    return jnp.concatenate(stack, axis=0)


def dot(left, right):
    return jnp.dot(left, right, preferred_element_type=jnp.float32)


def kernel(
    n, tiles, offsets, slot,
    x_hbm, idx_hbm, val_hbm, var_hbm, loc_hbm, out_ref,
    x, idx, val, var, loc, hs1, hr1, s1, r1, s2, r2, hs2, hr2,
    in_sem, hs1_sem, hr1_sem, s1_sem, r1_sem, s2_sem, r2_sem, hs2_sem, hr2_sem,
):
    me = lax.axis_index("mem")
    mt = lax.axis_index("tile")
    _, local, rows, width = x.shape
    members = n * local
    per_row = rows // 8

    loads = [
        pltpu.make_async_copy(src, dst, in_sem.at[i])
        for i, (src, dst) in enumerate(
            ((x_hbm, x), (idx_hbm, idx), (val_hbm, val), (var_hbm, var), (loc_hbm, loc))
        )
    ]
    for load in loads:
        load.start()

    def peers(body):
        def step(i, carry):
            body(lax.rem(me + i, n))
            return carry

        lax.fori_loop(1, n, step, 0, unroll=n <= 16)

    barrier = pltpu.get_barrier_semaphore()
    neighbours = [lax.rem(mt + d, tiles) for d in offsets]
    for t in neighbours:
        pl.semaphore_signal(barrier, inc=1, device_id=(me, t), device_id_type=MESH)
    peers(lambda p: pl.semaphore_signal(barrier, inc=1, device_id=(p, mt), device_id_type=MESH))

    lane = lax.broadcasted_iota(jnp.int32, (8, 128), 1)
    lane_rows = lax.broadcasted_iota(jnp.int32, (rows, 128), 1)
    lane_n = lax.broadcasted_iota(jnp.int32, (n, 128), 1)

    loads[0].wait()
    chunks = [(v, m, r) for v in range(3) for m in range(local) for r in range(per_row)]
    for block in range(hs1.shape[0]):
        packed = jnp.zeros((8, 128), jnp.float32)
        for g, (v, m, r) in enumerate(chunks[block * 16 : block * 16 + 16]):
            rolled = pltpu.roll(x[v, m, r * 8 : r * 8 + 8, :], (HALO + 8 * g) % 128, 1)
            packed = jnp.where((lane >= 8 * g) & (lane < 8 * g + 8), rolled, packed)
        hs1[block] = packed

    pl.semaphore_wait(barrier, n - 1 + len(offsets))

    halo_copies = [
        pltpu.make_async_remote_copy(
            src_ref=hs1, dst_ref=hr1.at[i], send_sem=hs1_sem.at[i], recv_sem=hr1_sem.at[i],
            device_id=(me, t), device_id_type=MESH,
        )
        for i, t in enumerate(neighbours)
    ]
    for copy in halo_copies:
        copy.start()

    for load in loads[1:]:
        load.wait()
    nobs = idx.shape[2]
    which = idx[0]
    entry = lax.broadcasted_iota(jnp.int32, (3 * PCELL, nobs), 0)
    picks = jnp.where(entry == which, 1.0, 0.0).astype(jnp.bfloat16)
    weight = loc[0] / var[0]

    for copy in halo_copies:
        copy.wait_recv()

    def edge_tile(sources, g, mask_lane):
        shift = (128 - HALO - 8 * g) % 128
        if len(sources) == 1:
            rolled = pltpu.roll(sources[0], shift, 1)
            return jnp.where((mask_lane < HALO) | (mask_lane >= 128 - HALO), rolled, 0.0)
        left = pltpu.roll(sources[0], shift, 1)
        right = pltpu.roll(sources[1], shift, 1)
        return jnp.where(mask_lane < HALO, right, jnp.where(mask_lane >= 128 - HALO, left, 0.0))

    for m in range(local):
        fields = []
        for v in range(3):
            edges = []
            for r in range(per_row):
                c = (v * local + m) * per_row + r
                sources = [hr1[i, c // 16] for i in range(len(offsets))]
                edges.append(edge_tile(sources, c % 16, lane))
            edge = edges[0] if per_row == 1 else jnp.concatenate(edges, axis=0)
            fields.append(jnp.concatenate([x[v, m], edge], axis=1))
        for v, field in enumerate(advance(fields)):
            s1[pl.ds(v * local + m, rows, stride=slot), :] = field[:, :128]

    def at_slot(ref, p):
        return ref.at[pl.ds(pl.multiple_of(p * slot, 8), slot), :]

    def own(source, target):
        where = pl.ds(pl.multiple_of(me * slot, 8), slot)
        target[where, :] = source[where, :]

    def row_copy(p, source, target, send_sem, recv_sem):
        return pltpu.make_async_remote_copy(
            src_ref=at_slot(source, p), dst_ref=at_slot(target, me),
            send_sem=send_sem, recv_sem=recv_sem, device_id=(p, mt), device_id_type=MESH,
        )

    def wait_slots(ref, sem):
        part = ref.at[pl.ds(0, (n - 1) * slot), :]
        pltpu.make_async_copy(part, part, sem).wait()

    peers(lambda p: row_copy(p, s1, r1, s1_sem, r1_sem).start())
    own(s1, r1)
    wait_slots(r1, r1_sem)

    state = jnp.concatenate(
        [
            jnp.concatenate([r1[pl.ds(v * local + m, n, stride=slot), :] for m in range(local)], axis=0)
            for v in range(3)
        ],
        axis=1,
    )
    seen = dot(jnp.concatenate(pieces(state), axis=0), picks)
    seen = seen[:members] + (seen[members : 2 * members] + seen[2 * members :])
    ybar = jnp.mean(seen, axis=0, keepdims=True)
    yp = seen - ybar
    yr = yp * weight
    rep = 128 // members
    yp_parts = [jnp.concatenate([p] * rep, axis=0) for p in pieces(yp)]
    yr_parts = pieces(yr)
    gram = None
    for b in (2, 1, 0):
        lefts = yr_parts[: 3 - b]
        left = lefts[0] if len(lefts) == 1 else jnp.concatenate(lefts, axis=0)
        full = lax.dot_general(
            left, yp_parts[b], (((1,), (1,)), ((), ())), preferred_element_type=jnp.float32
        )
        for a in range(len(lefts) - 1, -1, -1):
            part = full[a * members : (a + 1) * members]
            gram = part if gram is None else gram + part
    row_id = lax.broadcasted_iota(jnp.int32, (members, 128), 0)
    col_id = lax.rem(lax.broadcasted_iota(jnp.int32, (members, 128), 1), members)
    identity = jnp.where(row_id == col_id, 1.0, 0.0)
    amat = gram + (members - 1.0) * identity
    square = jnp.sum(jnp.sum(amat * amat, axis=0, keepdims=True), axis=1, keepdims=True)
    frob = jnp.sqrt(square * (1.0 / rep))
    inverse = 1.0 / frob

    xbar = jnp.mean(state, axis=0, keepdims=True)
    pert = state - xbar
    innov = val[0] - ybar
    projected = jnp.sum(yr * innov, axis=1, keepdims=True)
    carried = jnp.concatenate([pert, jnp.broadcast_to(projected, (members, 128))], axis=1)

    ymat = amat * inverse
    newton = 1.5 * identity - 0.5 * ymat
    ymat = dot(left_factor(newton, members), right_factor(ymat, members))
    zmat = newton
    for step in range(1, NSIT):
        zleft = left_factor(zmat, members)
        newton = 1.5 * identity - 0.5 * dot(zleft, right_factor(ymat, members))
        nleft = left_factor(newton, members)
        if step < NSIT - 1:
            both = dot(nleft, right_factor(jnp.concatenate([ymat, zmat], axis=1), members))
            ymat, zmat = both[:, :128], both[:, 128:]
        else:
            carried = dot(zleft, right_factor(carried, members))
            carried = dot(nleft, right_factor(carried, members))
    moved = carried[:, : 3 * PCELL]
    gain = carried[:, 3 * PCELL : 3 * PCELL + 1]
    shift = xbar + jnp.sum(moved * gain, axis=0, keepdims=True) * inverse
    updated = shift + jnp.sqrt((members - 1.0) * inverse) * moved

    packed = jnp.zeros((n, 128), jnp.float32)
    for v in range(3):
        for m in range(local):
            part = updated[m * n : (m + 1) * n, v * PCELL : (v + 1) * PCELL]
            k = v * local + m
            s2[pl.ds(k, n, stride=slot), :] = part
            rolled = pltpu.roll(part, (HALO + 8 * k) % 128, 1)
            packed = jnp.where((lane_n >= 8 * k) & (lane_n < 8 * k + 8), rolled, packed)
    for p in range(n):
        hs2[p] = packed[p : p + 1]

    def edge_copy(p, i):
        return pltpu.make_async_remote_copy(
            src_ref=hs2.at[p], dst_ref=hr2.at[i, me], send_sem=hs2_sem.at[i], recv_sem=hr2_sem.at[i],
            device_id=(p, neighbours[i]), device_id_type=MESH,
        )

    for i in range(len(offsets)):
        peers(lambda p: edge_copy(p, i).start())
        edge_copy(me, i).start()
    peers(lambda p: row_copy(p, s2, r2, s2_sem, r2_sem).start())
    own(s2, r2)

    for copy in halo_copies:
        copy.wait_send()
    wait_slots(s1, s1_sem)

    wait_slots(r2, r2_sem)
    for i in range(len(offsets)):
        pltpu.make_async_copy(hr2.at[i], hr2.at[i], hr2_sem.at[i]).wait()
    sources = [
        jnp.concatenate([hr2[i, r] for r in range(rows)], axis=0) for i in range(len(offsets))
    ]
    for m in range(local):
        fields = []
        for v in range(3):
            k = v * local + m
            edge = edge_tile(sources, k, lane_rows)
            fields.append(jnp.concatenate([r2[pl.ds(k, rows, stride=slot), :], edge], axis=1))
        for v, field in enumerate(advance(fields)):
            out_ref[v, m] = field[:, :128]

    wait_slots(s2, s2_sem)
    for i in range(len(offsets)):
        pltpu.make_async_copy(hs2, hs2, hs2_sem.at[i]).wait()


def local(n, tiles, member_perturbations, obs_index, obs_value, obs_var, loc_weight):
    x = member_perturbations
    _, count, rows, width = x.shape
    assert width == PCELL and rows == n and rows % 8 == 0
    assert obs_index.shape[:2] == (1, 1) and 128 % (n * count) == 0 and 24 * count <= 128
    slot = -(-3 * count // 8) * 8
    offsets = (1,) if tiles == 2 else (1, tiles - 1)
    blocks = -(-3 * count * (rows // 8) // 16)
    obs = obs_index.shape
    f32 = jnp.float32
    dma = pltpu.SemaphoreType.DMA
    sides = len(offsets)
    return pl.pallas_call(
        functools.partial(kernel, n, tiles, offsets, slot),
        out_shape=jax.ShapeDtypeStruct(x.shape, f32),
        in_specs=[pl.BlockSpec(memory_space=pl.ANY)] * 5,
        out_specs=pl.BlockSpec(memory_space=pltpu.VMEM),
        scratch_shapes=[
            pltpu.VMEM(x.shape, f32),
            pltpu.VMEM(obs, jnp.int32),
            pltpu.VMEM(obs, f32),
            pltpu.VMEM(obs, f32),
            pltpu.VMEM(obs, f32),
            pltpu.VMEM((blocks, 8, 128), f32),
            pltpu.VMEM((sides, blocks, 8, 128), f32),
            pltpu.VMEM((rows * slot, 128), f32),
            pltpu.VMEM((n * slot, 128), f32),
            pltpu.VMEM((n * slot, 128), f32),
            pltpu.VMEM((rows * slot, 128), f32),
            pltpu.VMEM((n, 1, 128), f32),
            pltpu.VMEM((sides, rows, 1, 128), f32),
            dma((5,)),
            dma((sides,)),
            dma((sides,)),
            dma,
            dma,
            dma,
            dma,
            dma((sides,)),
            dma((sides,)),
        ],
        compiler_params=pltpu.CompilerParams(collective_id=0, has_side_effects=True),
        name="cycle",
    )(x, obs_index, obs_value, obs_var, loc_weight)


def solution(mesh):
    in_specs = (
        P(None, "mem", None, "tile"),
        P("mem", "tile", None),
        P("mem", "tile", None),
        P("mem", "tile", None),
        P("mem", "tile", None),
    )
    out_specs = P(None, "mem", None, "tile")
    body = functools.partial(local, mesh.shape["mem"], mesh.shape["tile"])
    return jax.shard_map(body, mesh=mesh, in_specs=in_specs, out_specs=out_specs, check_vma=False)
```

time: 52.7 us -> 23.3 us (0.44)
  Pallas kernels: 0 us -> 21.6 us
  waiting for transfers between devices: 12.8 us -> 0 us
  starting transfers between devices: 11.1 us -> 0 us
  blocking collectives: 9.34 us -> 0 us
  local copies, waits for them, and re-layouts: 9.04 us -> 1.42 us
  matrix products: 4.63 us -> 0 us
  other arithmetic: 4.22 us -> 0 us
  between operations: 1.26 us -> 0.01 us
    pallas_call x0 -> x1, Pallas kernels: none -> 21.6 us  [local(): pl.pallas_call(functools.partial(kernel, n, tiles, offsets, slot), out_sh...]
    all_to_all x1 -> x0, blocking collectives: 9.34 us -> none  [local(): lax.all_to_all(updated_member_set.reshape(3, members, row_count, columns)...]
    all_to_all x1 -> x0, waiting for transfers between devices: 6.88 us -> none  [local(): lax.all_to_all(background_member_set, 'mem', split_axis=2, concat_axis=1,...]
    slice x64 -> x0, local copies, waits for them, and re-layouts: 5.97 us -> none  [the longest x62 4.91 us: along(): return (jnp.roll(inner, -1, -2) - jnp.roll(inner, 1, -2)) * 0.5]
    all_to_all x1 -> x0, starting transfers between devices: 5.94 us -> none  [local(): lax.all_to_all(background_member_set, 'mem', split_axis=2, concat_axis=1,...]
    ppermute x4 -> x0, waiting for transfers between devices: 5.91 us -> none  [the longest x2 3.35 us: with_halo(): lax.ppermute(tail, axis, [(i, (i + 1) % count) for i in range(count)])]
    ppermute x4 -> x0, starting transfers between devices: 5.14 us -> none  [the longest x2 3.57 us: with_halo(): lax.ppermute(tail, axis, [(i, (i + 1) % count) for i in range(count)])]
    dot_general x22 -> x0, matrix products: 4.63 us -> none  [the longest x18 2.66 us: product(): return jnp.einsum('rbij,rbjk->rbik', left, right, precision=highest)]
  transfers between devices with their start and end apart: 5 -> 0, of which waited for: 5 -> 0; matrix products, arithmetic and copies ran while one was open for 0% -> 0% of each run, Pallas kernels for 0% -> 0%
where the time goes in v1:
time: 23.3 us; the launch traced here: 23.1 us
  Pallas kernels  21.6 us (93%)
  local copies, waits for them, and re-layouts  1.42 us (6%)
    pallas_call x1, Pallas kernels, local(): pl.pallas_call(functools.partial(kernel, n, tiles, offsets, slot), out_sh...  21.6 us
    unnamed x1, local copies, waits for them, and re-layouts  1.42 us

profile of v1, /device:TPU:0, one launch (start us, length us, event | category | flops | bytes accessed | tf_op | source)
XLA Modules:
  0.0 23.1 jit_solution(13341720738046068666)
XLA Ops:
  0.0 21.6 %cycle.1 = f32[3,2,16,128]{3,2,1,0:T(8,128)} custom-call(f32[3,2,16,128]{3,2,1,0:T(8,128)} %x_hbm.1, s32[1,1,256]{2,1,0:T(1,128)} %idx_hbm.1, f32[1,1,256]{2,1,0:T(1,128)} %val_hbm.1, f32[1,1,256]{2,1,0:T(1,128)} %var_hbm.1, f32[1,1,256]{2,1,0:T(1,128)} %loc_hbm.1), custom_call_target="tpu_custom_call" | custom-call | tf_op jit(solution)/shard_map/cycle/pallas_call | solution.py:322
  21.6 1.4 %copy.7 = f32[3,2,16,128]{3,2,1,0:T(8,128)} copy(f32[3,2,16,128]{3,2,1,0:T(8,128)} %cycle.1) | data formatting | bytes 98304

commit v2 on v1

--- a/solution.py
+++ b/solution.py
@@ -93,7 +93,7 @@
     n, tiles, offsets, slot,
     x_hbm, idx_hbm, val_hbm, var_hbm, loc_hbm, out_ref,
     x, idx, val, var, loc, hs1, hr1, s1, r1, s2, r2, hs2, hr2,
-    in_sem, hs1_sem, hr1_sem, s1_sem, r1_sem, s2_sem, r2_sem, hs2_sem, hr2_sem,
+    in_sem, hs1_sem, hr1_sem, s1_sem, r1_sem, s2_sem, r2_sem, hs2_sem, hr2_sem, told_sem,
 ):
     me = lax.axis_index("mem")
     mt = lax.axis_index("tile")
@@ -119,9 +119,20 @@
 
     barrier = pltpu.get_barrier_semaphore()
     neighbours = [lax.rem(mt + d, tiles) for d in offsets]
+    odd = lax.rem(me, 2)
+    even_one = me - odd
+    partner = me + 1 - 2 * odd
     for t in neighbours:
-        pl.semaphore_signal(barrier, inc=1, device_id=(me, t), device_id_type=MESH)
-    peers(lambda p: pl.semaphore_signal(barrier, inc=1, device_id=(p, mt), device_id_type=MESH))
+        pl.semaphore_signal(barrier, inc=1, device_id=(even_one, t), device_id_type=MESH)
+
+    pl.semaphore_signal(barrier, inc=1, device_id=(partner, mt), device_id_type=MESH)
+
+    def greet(i, carry):
+        p = lax.rem(even_one + 2 * i, n) + 1
+        pl.semaphore_signal(barrier, inc=1, device_id=(p, mt), device_id_type=MESH)
+        return carry
+
+    lax.fori_loop(1, n // 2, greet, 0, unroll=n <= 16)
 
     lane = lax.broadcasted_iota(jnp.int32, (8, 128), 1)
     lane_rows = lax.broadcasted_iota(jnp.int32, (rows, 128), 1)
@@ -136,7 +147,14 @@
             packed = jnp.where((lane >= 8 * g) & (lane < 8 * g + 8), rolled, packed)
         hs1[block] = packed
 
-    pl.semaphore_wait(barrier, n - 1 + len(offsets))
+    @pl.when(odd == 0)
+    def _():
+        pl.semaphore_wait(barrier, 1 + 2 * len(offsets))
+        pl.semaphore_signal(told_sem, inc=1, device_id=(partner, mt), device_id_type=MESH)
+
+    @pl.when(odd == 1)
+    def _():
+        pl.semaphore_wait(told_sem, 1)
 
     halo_copies = [
         pltpu.make_async_remote_copy(
@@ -197,6 +215,15 @@
     def wait_slots(ref, sem):
         part = ref.at[pl.ds(0, (n - 1) * slot), :]
         pltpu.make_async_copy(part, part, sem).wait()
+
+    @pl.when(odd == 1)
+    def _():
+        pl.semaphore_wait(barrier, n - 1)
+        pl.semaphore_signal(told_sem, inc=1, device_id=(partner, mt), device_id_type=MESH)
+
+    @pl.when(odd == 0)
+    def _():
+        pl.semaphore_wait(told_sem, 1)
 
     peers(lambda p: row_copy(p, s1, r1, s1_sem, r1_sem).start())
     own(s1, r1)
@@ -310,7 +337,7 @@
 def local(n, tiles, member_perturbations, obs_index, obs_value, obs_var, loc_weight):
     x = member_perturbations
     _, count, rows, width = x.shape
-    assert width == PCELL and rows == n and rows % 8 == 0
+    assert width == PCELL and rows == n and rows % 8 == 0 and n % 2 == 0
     assert obs_index.shape[:2] == (1, 1) and 128 % (n * count) == 0 and 24 * count <= 128
     slot = -(-3 * count // 8) * 8
     offsets = (1,) if tiles == 2 else (1, tiles - 1)
@@ -347,6 +374,7 @@
             dma,
             dma((sides,)),
             dma((sides,)),
+            pltpu.SemaphoreType.REGULAR,
         ],
         compiler_params=pltpu.CompilerParams(collective_id=0, has_side_effects=True),
         name="cycle",

time: 23.3 us -> 20.5 us (0.88)
  Pallas kernels: 21.6 us -> 18.9 us
    pallas_call x1, Pallas kernels: 21.6 us -> 18.9 us  [local(): pl.pallas_call(functools.partial(kernel, n, tiles, offsets, slot), out_sh...]
where the time goes in v2:
time: 20.5 us; the launch traced here: 20.3 us
  Pallas kernels  18.9 us (92%)
  local copies, waits for them, and re-layouts  1.42 us (7%)
    pallas_call x1, Pallas kernels, local(): pl.pallas_call(functools.partial(kernel, n, tiles, offsets, slot), out_sh...  18.9 us
    unnamed x1, local copies, waits for them, and re-layouts  1.42 us

profile of v2, /device:TPU:0, one launch (start us, length us, event | category | flops | bytes accessed | tf_op | source)
XLA Modules:
  0.0 20.3 jit_solution(3032942445184316153)
XLA Ops:
  0.0 18.9 %cycle.1 = f32[3,2,16,128]{3,2,1,0:T(8,128)} custom-call(f32[3,2,16,128]{3,2,1,0:T(8,128)} %x_hbm.1, s32[1,1,256]{2,1,0:T(1,128)} %idx_hbm.1, f32[1,1,256]{2,1,0:T(1,128)} %val_hbm.1, f32[1,1,256]{2,1,0:T(1,128)} %var_hbm.1, f32[1,1,256]{2,1,0:T(1,128)} %loc_hbm.1), custom_call_target="tpu_custom_call" | custom-call | tf_op jit(solution)/shard_map/cycle/pallas_call | solution.py:349
  18.9 1.4 %copy.7 = f32[3,2,16,128]{3,2,1,0:T(8,128)} copy(f32[3,2,16,128]{3,2,1,0:T(8,128)} %cycle.1) | data formatting | bytes 98304

commit v3 on v2

--- a/solution.py
+++ b/solution.py
@@ -89,10 +89,20 @@
     return jnp.dot(left, right, preferred_element_type=jnp.float32)
 
 
+def edge_tile(sources, g, mask_lane):
+    shift = (128 - HALO - 8 * g) % 128
+    if len(sources) == 1:
+        rolled = pltpu.roll(sources[0], shift, 1)
+        return jnp.where((mask_lane < HALO) | (mask_lane >= 128 - HALO), rolled, 0.0)
+    left = pltpu.roll(sources[0], shift, 1)
+    right = pltpu.roll(sources[1], shift, 1)
+    return jnp.where(mask_lane < HALO, right, jnp.where(mask_lane >= 128 - HALO, left, 0.0))
+
+
 def kernel(
     n, tiles, offsets, slot,
-    x_hbm, idx_hbm, val_hbm, var_hbm, loc_hbm, out_ref,
-    x, idx, val, var, loc, hs1, hr1, s1, r1, s2, r2, hs2, hr2,
+    x_hbm, idx_hbm, val_hbm, var_hbm, loc_hbm, r2, hr2,
+    x, idx, val, var, loc, hs1, hr1, s1, r1, s2, hs2,
     in_sem, hs1_sem, hr1_sem, s1_sem, r1_sem, s2_sem, r2_sem, hs2_sem, hr2_sem, told_sem,
 ):
     me = lax.axis_index("mem")
@@ -135,7 +145,6 @@
     lax.fori_loop(1, n // 2, greet, 0, unroll=n <= 16)
 
     lane = lax.broadcasted_iota(jnp.int32, (8, 128), 1)
-    lane_rows = lax.broadcasted_iota(jnp.int32, (rows, 128), 1)
     lane_n = lax.broadcasted_iota(jnp.int32, (n, 128), 1)
 
     loads[0].wait()
@@ -176,15 +185,6 @@
 
     for copy in halo_copies:
         copy.wait_recv()
-
-    def edge_tile(sources, g, mask_lane):
-        shift = (128 - HALO - 8 * g) % 128
-        if len(sources) == 1:
-            rolled = pltpu.roll(sources[0], shift, 1)
-            return jnp.where((mask_lane < HALO) | (mask_lane >= 128 - HALO), rolled, 0.0)
-        left = pltpu.roll(sources[0], shift, 1)
-        right = pltpu.roll(sources[1], shift, 1)
-        return jnp.where(mask_lane < HALO, right, jnp.where(mask_lane >= 128 - HALO, left, 0.0))
 
     for m in range(local):
         fields = []
@@ -308,18 +308,37 @@
         peers(lambda p: edge_copy(p, i).start())
         edge_copy(me, i).start()
     peers(lambda p: row_copy(p, s2, r2, s2_sem, r2_sem).start())
-    own(s2, r2)
+    keep = pltpu.make_async_copy(at_slot(s2, me), at_slot(r2, me), in_sem.at[0])
+    keep.start()
 
     for copy in halo_copies:
         copy.wait_send()
     wait_slots(s1, s1_sem)
 
+    keep.wait()
     wait_slots(r2, r2_sem)
     for i in range(len(offsets)):
         pltpu.make_async_copy(hr2.at[i], hr2.at[i], hr2_sem.at[i]).wait()
+    wait_slots(s2, s2_sem)
+    for i in range(len(offsets)):
+        pltpu.make_async_copy(hs2, hs2, hs2_sem.at[i]).wait()
+
+
+def finish(slot, r2_hbm, hr2_hbm, out_hbm, r2, hr2, out, in_sem, out_sem):
+    loads = [
+        pltpu.make_async_copy(r2_hbm, r2, in_sem.at[0]),
+        pltpu.make_async_copy(hr2_hbm, hr2, in_sem.at[1]),
+    ]
+    for load in loads:
+        load.start()
+    for load in loads:
+        load.wait()
+    _, local, rows, _ = out.shape
+    lane_rows = lax.broadcasted_iota(jnp.int32, (rows, 128), 1)
     sources = [
-        jnp.concatenate([hr2[i, r] for r in range(rows)], axis=0) for i in range(len(offsets))
+        jnp.concatenate([hr2[i, r] for r in range(rows)], axis=0) for i in range(hr2.shape[0])
     ]
+    stores = []
     for m in range(local):
         fields = []
         for v in range(3):
@@ -327,11 +346,11 @@
             edge = edge_tile(sources, k, lane_rows)
             fields.append(jnp.concatenate([r2[pl.ds(k, rows, stride=slot), :], edge], axis=1))
         for v, field in enumerate(advance(fields)):
-            out_ref[v, m] = field[:, :128]
-
-    wait_slots(s2, s2_sem)
-    for i in range(len(offsets)):
-        pltpu.make_async_copy(hs2, hs2, hs2_sem.at[i]).wait()
+            out[v, m] = field[:, :128]
+            stores.append(pltpu.make_async_copy(out.at[v, m], out_hbm.at[v, m], out_sem.at[m, v]))
+            stores[-1].start()
+    for store in stores:
+        store.wait()
 
 
 def local(n, tiles, member_perturbations, obs_index, obs_value, obs_var, loc_weight):
@@ -346,11 +365,15 @@
     f32 = jnp.float32
     dma = pltpu.SemaphoreType.DMA
     sides = len(offsets)
-    return pl.pallas_call(
+    hbm = pl.BlockSpec(memory_space=pl.ANY)
+    rows_back, edges_back = pl.pallas_call(
         functools.partial(kernel, n, tiles, offsets, slot),
-        out_shape=jax.ShapeDtypeStruct(x.shape, f32),
-        in_specs=[pl.BlockSpec(memory_space=pl.ANY)] * 5,
-        out_specs=pl.BlockSpec(memory_space=pltpu.VMEM),
+        out_shape=(
+            jax.ShapeDtypeStruct((rows * slot, 128), f32),
+            jax.ShapeDtypeStruct((sides, rows, 1, 128), f32),
+        ),
+        in_specs=[hbm] * 5,
+        out_specs=(hbm, hbm),
         scratch_shapes=[
             pltpu.VMEM(x.shape, f32),
             pltpu.VMEM(obs, jnp.int32),
@@ -362,9 +385,7 @@
             pltpu.VMEM((rows * slot, 128), f32),
             pltpu.VMEM((n * slot, 128), f32),
             pltpu.VMEM((n * slot, 128), f32),
-            pltpu.VMEM((rows * slot, 128), f32),
             pltpu.VMEM((n, 1, 128), f32),
-            pltpu.VMEM((sides, rows, 1, 128), f32),
             dma((5,)),
             dma((sides,)),
             dma((sides,)),
@@ -379,6 +400,20 @@
         compiler_params=pltpu.CompilerParams(collective_id=0, has_side_effects=True),
         name="cycle",
     )(x, obs_index, obs_value, obs_var, loc_weight)
+    return pl.pallas_call(
+        functools.partial(finish, slot),
+        out_shape=jax.ShapeDtypeStruct(x.shape, f32),
+        in_specs=[hbm, hbm],
+        out_specs=hbm,
+        scratch_shapes=[
+            pltpu.VMEM((rows * slot, 128), f32),
+            pltpu.VMEM((sides, rows, 1, 128), f32),
+            pltpu.VMEM(x.shape, f32),
+            dma((2,)),
+            dma((count, 3)),
+        ],
+        name="second_step",
+    )(rows_back, edges_back)
 
 
 def solution(mesh):

time: 20.5 us -> 20.1 us (0.980)
  local copies, waits for them, and re-layouts: 1.42 us -> 0 us
  Pallas kernels: 18.9 us -> 19.8 us
    pallas_call x0 -> x1, Pallas kernels: none -> 2.12 us  [local(): pl.pallas_call(functools.partial(finish, slot), out_shape=jax.ShapeDtypeS...]
    unnamed x1 -> x0, local copies, waits for them, and re-layouts: 1.42 us -> none
    pallas_call x1, Pallas kernels: 18.9 us -> 17.7 us  [local(): pl.pallas_call(functools.partial(kernel, n, tiles, offsets, slot), out_sh...]
where the time goes in v3:
time: 20.1 us; the launch traced here: 19.8 us
  Pallas kernels  19.8 us (99%)
    pallas_call x1, Pallas kernels, local(): pl.pallas_call(functools.partial(kernel, n, tiles, offsets, slot), out_sh...  17.7 us
    pallas_call x1, Pallas kernels, local(): pl.pallas_call(functools.partial(finish, slot), out_shape=jax.ShapeDtypeS...  2.12 us

profile of v3, /device:TPU:0, one launch (start us, length us, event | category | flops | bytes accessed | tf_op | source)
XLA Modules:
  0.0 19.8 jit_solution(10310356302631924567)
XLA Ops:
  0.0 17.7 %cycle.1 = (f32[128,128]{1,0:T(8,128)}, f32[1,16,1,128]{3,2,1,0:T(1,128)}) custom-call(f32[3,2,16,128]{3,2,1,0:T(8,128)} %x_hbm.1, s32[1,1,256]{2,1,0:T(1,128)} %idx_hbm.1, f32[1,1,256]{2,1,0:T(1,128)} %val_hbm.1, f32[1,1,256]{2,1,0:T(1,128)} %var_hbm.1, f32[1,1,256]{2,1,0:T(1,128)} %loc_hbm.1), custom_call_target="tpu_custom_call" | custom-call | tf_op jit(solution)/shard_map/cycle/pallas_call | solution.py:369
  17.7 2.1 %second_step.1 = f32[3,2,16,128]{3,2,1,0:T(8,128)} custom-call(f32[128,128]{1,0:T(8,128)} %get-tuple-element.7.r2_hbm, f32[1,16,1,128]{3,2,1,0:T(1,128)} %get-tuple-element.8.hr2_hbm), custom_call_target="tpu_custom_call" | custom-call | tf_op jit(solution)/shard_map/second_step/pallas_call | solution.py:403
